TPU v7x, 256 devices: a whole 4x4x8 slice. The times are simulated.
256 devices in a mesh: rows: 64 (over x, z, core), cols: 4 (over y).
Axes of the slice: x: 4, y: 4, z: 8, core: 2. Of those that a mesh axis runs over, the one named last changes fastest.
Arguments:
- slot_tile: int32 [64, 3], replicated, may hold values from 0 to 128, as said below
- slot_ranks: int32 [64, 3, 4], P('rows', None, 'cols'), may hold values from 0 to 256, as said below
- diag_ranks: int32 [4], P('cols'), may hold values from 32 to 256
- panel_left_factors: bfloat16 [4, 192, 1024, 256], P('cols', 'rows'), may hold values from -12 to 12
- panel_v: bfloat16 [4, 192, 1024, 256], P('cols', 'rows'), may hold values from -0.1875 to 0.1875
- diag_u: bfloat16 [4, 1024, 256], P('cols'), may hold values from -0.38 to 0.38, as said below
- diag_v: bfloat16 [4, 1024, 256], P('cols'), may hold values from -1 to 1
- panel_points: int32 [192, 2, 1024], P('rows', None, 'cols'), may hold values from 0 to 1023, as said below
- diag_points: int32 [2, 1024], replicated, may hold values from 0 to 1023, as said below
- rhs_diag: float32 [1024, 512], P(None, 'cols'), may hold values from -0.3 to 0.3
- rhs_rest: float32 [128, 4, 4, 64, 512], P(None, 'cols', None, 'rows'), may hold values from -6 to 6
Outputs:
- panel_factor: bfloat16 [192, 1024, 1024], P('rows', 'cols')
- diag_solution: float32 [1024, 512], P(None, 'cols')
- rhs_out: float32 [128, 4, 4, 64, 512], P(None, 'cols', None, 'rows')
Inputs may be any that keep to these rules, and one draw needn't show every extreme that they name: `slot_tile`: every tile 0 to 127 stands in exactly one slot; 128 marks an empty slot; the live slots of an owner come first; every owner has 1 to 3 live slots and some owner has 3. Owners are chosen by the tiles' summed ranks. `slot_ranks`: live slots have ranks 32 to 256, empty slots 0; both 32 and 256 occur. The columns of each diag_u[j] are orthogonal, with lengths 0.1 to 0.38. `panel_points`: row 0 holds x, row 1 holds y. A live slot holds the cells of a block of 32 x (32) grid cells in some order; blocks of different tiles and of the diagonal tile are distinct; an empty slot holds the points of some tile. `diag_points`: row 0 holds x, row 1 holds y: the cells of one block of 32 x (32) grid cells in some order.
All inputs are finite; a program needn't handle non-finite values.
Results may differ from a plain program's by a relative error of at most 0.0057.
Values may be sent and summed in bfloat16 or wider, within the bound.
A program may use at most 128 MiB of HBM per device.

v0:
```python
import jax
import jax.numpy as jnp
from jax import lax
from jax.sharding import PartitionSpec as P

GX = 1024
length_scale = 0.3
nugget = 1.0


def matern(first_x, first_y, second_x, second_y):
    spacing = 1.0 / GX
    delta_x = (first_x - second_x) * spacing
    delta_y = (first_y - second_y) * spacing
    scaled = jnp.sqrt(3.0) * jnp.sqrt(delta_x * delta_x + delta_y * delta_y) / length_scale
    return (1.0 + scaled) * jnp.exp(-scaled)


def owner_rows(slot_tile, tile_count, per_peer, row_devices):
    flat_tiles = slot_tile.reshape(-1)
    slot_count = flat_tiles.shape[0]
    tmax_local = slot_tile.shape[1]
    owner_slot = (
        jnp.zeros((tile_count + 1,), jnp.int32)
        .at[flat_tiles]
        .set(jnp.arange(slot_count, dtype=jnp.int32))[:tile_count]
    )
    source_row = owner_slot // tmax_local
    source_place = owner_slot % tmax_local
    step_index = jnp.arange(per_peer, dtype=jnp.int32)
    return (
        (source_place[:, None] * per_peer + step_index[None, :]) * row_devices + source_row[:, None]
    ).reshape(-1)


def times_block(owned_rows, forward):
    return jnp.dot(
        owned_rows,
        lax.all_gather(forward, "cols", axis=1, tiled=True),
        preferred_element_type=jnp.float32,
    )


def per_device(
    slot_tile,
    slot_ranks,
    diag_ranks,
    panel_left_factors,
    panel_v,
    diag_u,
    diag_v,
    panel_points,
    diag_points,
    rhs_diag,
    rhs_rest,
):
    row_devices = lax.axis_size("rows")
    col_devices = lax.axis_size("cols")
    slot_count = panel_left_factors.shape[1]
    tile_order = diag_u.shape[1]
    rank_max = diag_u.shape[2]
    quarter = tile_order // col_devices
    per_peer = quarter // row_devices
    tile_count = rhs_rest.shape[0]
    row_index = lax.axis_index("rows")
    rank_index = jnp.arange(rank_max, dtype=jnp.int32)
    diag_mask = (rank_index < diag_ranks[0]).astype(jnp.bfloat16)
    diagonal_left_factor = diag_u[0] * diag_mask[None, :]
    diagonal_right_factor = diag_v[0] * diag_mask[None, :]
    slot_mask = (rank_index[None, :] < slot_ranks[0, :, 0][:, None]).astype(jnp.bfloat16)
    slot_left_factor = panel_left_factors[0] * slot_mask[:, None, :]
    slot_right_factor = panel_v[0] * slot_mask[:, None, :]
    inner_product_core = jnp.einsum(
        "gok,oe->gke", slot_right_factor, diagonal_right_factor, preferred_element_type=jnp.float32
    ).astype(jnp.bfloat16)
    low_rows = jnp.einsum(
        "lgc,lcz->lgz", slot_left_factor, inner_product_core, preferred_element_type=jnp.float32
    ).astype(jnp.bfloat16)
    diag_core = jnp.einsum(
        "br,bq->rq",
        diagonal_right_factor,
        diagonal_right_factor,
        preferred_element_type=jnp.float32,
    ).astype(jnp.bfloat16)
    diag_low = jnp.dot(diagonal_left_factor, diag_core, preferred_element_type=jnp.float32).astype(
        jnp.bfloat16
    )
    gathered_low, gathered_left = (
        lax.all_gather(diag_low[None], "cols", axis=0, tiled=True),
        lax.all_gather(diagonal_left_factor[None], "cols", axis=0, tiled=True),
    )
    outgoing_low = low_rows.reshape(slot_count, col_devices, quarter, rank_max)
    update_term = jnp.einsum(
        "sjnr,jbr->snb",
        lax.all_to_all(outgoing_low, "cols", split_axis=1, concat_axis=1, tiled=True),
        gathered_left,
        preferred_element_type=jnp.float32,
    )
    centre = diag_points.astype(jnp.float32)
    identity = jnp.eye(tile_order, dtype=jnp.float32)
    diag_term = jnp.einsum(
        "jbr,jcr->bc", gathered_low, gathered_left, preferred_element_type=jnp.float32
    )
    own_block = matern(centre[0][:, None], centre[1][:, None], centre[0], centre[1])
    diag_system = own_block + nugget * identity - diag_term
    factor = jnp.linalg.cholesky(diag_system)
    inverse = jax.scipy.linalg.solve_triangular(factor, identity, lower=True)
    my_tiles = lax.dynamic_slice_in_dim(slot_tile, row_index, 1, 0)[0]
    live_mask = (my_tiles < tile_count).astype(jnp.float32)
    coords = panel_points.astype(jnp.float32)
    generated = matern(coords[:, 0, :, None], coords[:, 1, :, None], centre[0], centre[1])
    system_rows = live_mask[:, None, None] * (generated - update_term)
    panel_factor = jnp.einsum(
        "snb,cb->snc", system_rows, inverse, precision=lax.Precision.HIGHEST
    ).astype(jnp.bfloat16)
    diag_solution = jnp.dot(inverse, rhs_diag, precision=lax.Precision.HIGHEST)
    forward = diag_solution.astype(jnp.bfloat16)
    pick_rows = owner_rows(slot_tile, tile_count, per_peer, row_devices)
    outgoing_rows = panel_factor.reshape(slot_count, per_peer, row_devices, tile_order)
    incoming = lax.all_to_all(outgoing_rows, "rows", split_axis=2, concat_axis=2, tiled=True)
    owned_rows = jnp.take(incoming.reshape(-1, tile_order), pick_rows, axis=0)
    product = times_block(owned_rows, forward).astype(jnp.bfloat16)
    rhs_out = rhs_rest - product.reshape(rhs_rest.shape).astype(jnp.float32)
    return (panel_factor, diag_solution, rhs_out)


def solution(mesh):
    return jax.shard_map(
        per_device,
        mesh=mesh,
        in_specs=(
            P(),
            P("rows", None, "cols"),
            P("cols"),
            P("cols", "rows", None, None),
            P("cols", "rows", None, None),
            P("cols", None, None),
            P("cols", None, None),
            P("rows", None, "cols"),
            P(),
            P(None, "cols"),
            P(None, "cols", None, "rows", None),
        ),
        out_specs=(P("rows", "cols", None), P(None, "cols"), P(None, "cols", None, "rows", None)),
        check_vma=False,
    )
```

profile of v0, /device:TPU:1, one launch (start us, length us, event | category | flops | bytes accessed | tf_op | source)
XLA Modules:
  0.0 559.6 jit_solution(14840995524542032224)
XLA Ops:
  27.1 34.0 %all-gather.5.cloned.1.call-done = bf16[4,1024,256]{2,1,0:T(8,128)(2,1)} async-done(((bf16[1,1024,256]{2,1,0:T(8,128)(2,1)}), bf16[4,1024,256]{2,1,0:T(8,128)(2,1)}) %all-gather.5.cloned.1.call-update) | async-done | bytes 2097168 | tf_op jit(solution)/shard_map/all_gather | solution.py:90
  61.1 36.7 %all-gather.9.cloned.1.call-done = bf16[4096,256]{1,0:T(8,128)(2,1)} async-done(((bf16[1024,256]{1,0:T(8,128)(2,1)}), bf16[4096,256]{1,0:T(8,128)(2,1)}) %all-gather.9.cloned.1.call-update) | async-done | bytes 2097168 | tf_op jit(solution)/shard_map/all_gather | solution.py:89
  97.8 6.6 %convolution_bitcast_fusion = f32[1024,1024]{1,0:T(8,128)} fusion(bf16[4,1024,256]{2,1,0:T(8,128)(2,1)} %bitcast.174, bf16[4,1024,256]{2,1,0:T(8,128)(2,1)} %all-gather.5.cloned.1.call-done), kind=kOutput, calls=%fused_computation.28 | convolution fusion | flops 2147483648 | bytes 8388608 | tf_op jit(solution)/shard_map/jbr,jcr->bc/dot_general | solution.py:101
  109.7 9.6 %fusion.3 = f32[1024,1024]{1,0:T(8,128)S(1)} fusion(f32[1024,1024]{0,1:T(8,128)} %copy.22, f32[1024,1024]{1,0:T(8,128)} %convolution_bitcast_fusion, f32[1024]{0:T(1024)S(1)} %bitcast.169, f32[1024]{0:T(1024)S(1)} %bitcast.167), kind=kLoop, calls=%fused_computation.9 | loop fusion | flops 33554432 | bytes 12591104 | tf_op jit(solution)/shard_map/jit(cholesky)/div | solution.py:106
  121.3 11.7 %cholesky.224 = f32[128,128]{1,0:T(8,128)S(1)} custom-call(f32[128,128]{1,0:T(8,128)S(1)} %cholesky.583), custom_call_target="Cholesky" | custom-call | tf_op jit(solution)/shard_map/jit(cholesky)/cholesky | solution.py:106
  133.0 9.8 %custom-call.63 = f32[1,128,128]{1,2,0:T(8,128)S(1)} custom-call(f32[1,128,128]{2,1,0:T(8,128)S(1)} %get-tuple-element.67), custom_call_target="InvertDiagBlocksLowerTriangular" | custom-call | tf_op jit(solution)/shard_map/jit(cholesky)/cholesky | solution.py:106
  149.3 11.7 %cholesky.245 = f32[128,128]{1,0:T(8,128)S(1)} custom-call(f32[128,128]{1,0:T(8,128)S(1)} %cholesky.587), custom_call_target="Cholesky" | custom-call | tf_op jit(solution)/shard_map/jit(cholesky)/cholesky | solution.py:106
  161.6 10.2 %custom-call.64 = f32[1,128,128]{1,2,0:T(8,128)S(1)} custom-call(f32[1,128,128]{2,1,0:T(8,128)S(1)} %get-tuple-element.64), custom_call_target="InvertDiagBlocksLowerTriangular" | custom-call | tf_op jit(solution)/shard_map/jit(cholesky)/cholesky | solution.py:106
  175.2 11.7 %cholesky.470 = f32[128,128]{1,0:T(8,128)S(1)} custom-call(f32[128,128]{1,0:T(8,128)S(1)} %cholesky.592), custom_call_target="Cholesky" | custom-call | tf_op jit(solution)/shard_map/jit(cholesky)/cholesky | solution.py:106
  188.3 9.8 %custom-call.65 = f32[1,128,128]{1,2,0:T(8,128)S(1)} custom-call(f32[1,128,128]{2,1,0:T(8,128)S(1)} %get-tuple-element.61), custom_call_target="InvertDiagBlocksLowerTriangular" | custom-call | tf_op jit(solution)/shard_map/jit(cholesky)/cholesky | solution.py:106
  201.6 11.9 %cholesky.489 = f32[128,128]{1,0:T(8,128)S(1)} custom-call(f32[128,128]{1,0:T(8,128)S(1)} %cholesky.597), custom_call_target="Cholesky" | custom-call | tf_op jit(solution)/shard_map/jit(cholesky)/cholesky | solution.py:106
  214.8 9.8 %custom-call.66 = f32[1,128,128]{1,2,0:T(8,128)S(1)} custom-call(f32[1,128,128]{2,1,0:T(8,128)S(1)} %get-tuple-element.58), custom_call_target="InvertDiagBlocksLowerTriangular" | custom-call | tf_op jit(solution)/shard_map/jit(cholesky)/cholesky | solution.py:106
  228.1 11.7 %cholesky.508 = f32[128,128]{1,0:T(8,128)S(1)} custom-call(f32[128,128]{1,0:T(8,128)S(1)} %cholesky.602), custom_call_target="Cholesky" | custom-call | tf_op jit(solution)/shard_map/jit(cholesky)/cholesky | solution.py:106
  241.1 9.8 %custom-call.67 = f32[1,128,128]{1,2,0:T(8,128)S(1)} custom-call(f32[1,128,128]{2,1,0:T(8,128)S(1)} %get-tuple-element.55), custom_call_target="InvertDiagBlocksLowerTriangular" | custom-call | tf_op jit(solution)/shard_map/jit(cholesky)/cholesky | solution.py:106
  254.4 11.7 %cholesky.528 = f32[128,128]{1,0:T(8,128)S(1)} custom-call(f32[128,128]{1,0:T(8,128)S(1)} %cholesky.607), custom_call_target="Cholesky" | custom-call | tf_op jit(solution)/shard_map/jit(cholesky)/cholesky | solution.py:106
  267.5 9.8 %custom-call.68 = f32[1,128,128]{1,2,0:T(8,128)S(1)} custom-call(f32[1,128,128]{2,1,0:T(8,128)S(1)} %get-tuple-element.52), custom_call_target="InvertDiagBlocksLowerTriangular" | custom-call | tf_op jit(solution)/shard_map/jit(cholesky)/cholesky | solution.py:106
  280.3 11.7 %cholesky.548 = f32[128,128]{1,0:T(8,128)S(1)} custom-call(f32[128,128]{1,0:T(8,128)S(1)} %cholesky.612), custom_call_target="Cholesky" | custom-call | tf_op jit(solution)/shard_map/jit(cholesky)/cholesky | solution.py:106
  293.3 10.2 %custom-call.69 = f32[1,128,128]{1,2,0:T(8,128)S(1)} custom-call(f32[1,128,128]{2,1,0:T(8,128)S(1)} %get-tuple-element.49), custom_call_target="InvertDiagBlocksLowerTriangular" | custom-call | tf_op jit(solution)/shard_map/jit(cholesky)/cholesky | solution.py:106
  306.2 11.7 %cholesky.566 = f32[128,128]{1,0:T(8,128)S(1)} custom-call(f32[128,128]{1,0:T(8,128)S(1)} %convolution_subtract_fusion.11), custom_call_target="Cholesky" | custom-call | tf_op jit(solution)/shard_map/jit(cholesky)/cholesky | solution.py:106
  329.7 27.4 %while.1 = (s32[]{:T(128)}, f32[1024,1024]{1,0:T(8,128)}, s32[8,2]{0,1:T(2,128)S(1)}, f32[8,128,128]{2,1,0:T(8,128)}, s32[]{:T(128)}) while((s32[]{:T(128)}, f32[1024,1024]{1,0:T(8,128)}, s32[8,2]{0,1:T(2,128)S(1)}, f32[8,128,128]{2,1,0:T(8,128)}, s32[]{:T(128)}) %tuple.66), condition=%wide.while_cond, body=%wide.while_body.sunk | while | flops 2 | bytes 132705 | solution.py:107
  357.1 79.6 %custom-call.70 = f32[8,128,128]{1,2,0:T(8,128)S(1)} custom-call(f32[8,128,128]{2,1,0:T(8,128)} %get-tuple-element.10), custom_call_target="InvertDiagBlocksLowerTriangular" | custom-call | tf_op jit(solution)/shard_map/jit(_solve_triangular)/triangular_solve | solution.py:107
  469.6 16.3 %fusion.29 = bf16[3,256,1024]{2,1,0:T(8,128)(2,1)S(1)} fusion(f32[1024,1024]{1,0:T(8,128)} %convolution_dynamic-update-slice_fusion, f32[3,256,1024,1]{2,1,0,3:T(8,128)S(1)} %fusion.27, f32[1024]{0:T(1024)S(1)} %bitcast.170, f32[3,256]{1,0:T(4,128)S(1)} %get-tuple-element.84, f32[1024]{0:T(1024)S(1)} %bitcast.168, f32[3,256]{1,0:T(4,128)S(1)} %get-tuple-element.85, ...), kind=kOutput, calls=%fused_computation.40 | convolution fusion | flops 9674686464 | bytes 8927244 | tf_op jit(solution)/shard_map/snb,cb->snc/dot_general | solution.py:113
  489.4 11.0 %all-to-all-start.1 = ((bf16[3,4,64,1024]{3,1,0,2:T(4,128)(2,1)}), bf16[3,4,64,1024]{3,1,0,2:T(4,128)(2,1)}, u32[]{:S(2)}, u32[]{:S(2)}) async-start(bf16[3,4,64,1024]{3,1,0,2:T(4,128)(2,1)} %copy.24), calls=%async_computation.1 | async-start | bytes 3145728 | tf_op jit(solution)/shard_map/all_to_all | solution.py:120
  509.0 31.1 %all-to-all-done.1 = bf16[3,4,64,1024]{3,1,0,2:T(4,128)(2,1)} async-done(((bf16[3,4,64,1024]{3,1,0,2:T(4,128)(2,1)}), bf16[3,4,64,1024]{3,1,0,2:T(4,128)(2,1)}, u32[]{:S(2)}, u32[]{:S(2)}) %all-to-all-start.1) | async-done | bytes 1572896 | tf_op jit(solution)/shard_map/all_to_all | solution.py:120
  (144 shorter events, 151.1 us)
Async XLA Ops:
  7.2 493.5 %copy-start = (f32[1024,128]{1,0:T(8,128)S(1)}, f32[1024,128]{1,0:T(8,128)}, u32[]{:S(2)}) copy-start(f32[1024,128]{1,0:T(8,128)} %param.20) | copy-start | bytes 1572868
  7.2 5.9 %copy-start.9 = (bf16[1,1024,256]{2,1,0:T(8,128)(2,1)S(1)}, bf16[1,1024,256]{2,1,0:T(8,128)(2,1)}, u32[]{:S(2)}) copy-start(bf16[1,1024,256]{2,1,0:T(8,128)(2,1)} %param.17) | copy-start | bytes 1572868
  7.2 5.8 %copy-start.8 = (s32[1,3,1]{1,2,0:T(1,128)S(1)}, s32[1,3,1]{1,2,0:T(1,128)}, u32[]{:S(2)}) copy-start(s32[1,3,1]{1,2,0:T(1,128)} %param.12) | copy-start | bytes 40
  7.2 53.9 %all-gather.5.cloned.1.call-start = ((), (), s32[]{:S(2)}) async-start(), calls=%async_computation.2 | async-start | bytes 2621440 | tf_op jit(solution)/shard_map/all_gather | solution.py:90
  9.9 87.9 %all-gather.9.cloned.1.call-start = ((), (), s32[]{:S(2)}) async-start(), calls=%async_computation.4 | async-start | bytes 2621440 | tf_op jit(solution)/shard_map/all_gather | solution.py:89
  16.8 6.3 %copy-start.6 = (s32[2,1024]{1,0:T(2,128)S(1)}, s32[2,1024]{1,0:T(2,128)}, u32[]{:S(2)}) copy-start(s32[2,1024]{1,0:T(2,128)} %param.19) | copy-start | bytes 24580
  16.8 6.3 %copy-start.7 = (s32[3,2,256]{2,1,0:T(2,128)S(1)}, s32[3,2,256]{2,1,0:T(2,128)}, u32[]{:S(2)}) copy-start(s32[3,2,256]{2,1,0:T(2,128)} %param.18) | copy-start | bytes 18436
  16.8 6.3 %copy-start.5 = (s32[64,3]{0,1:T(4,128)S(1)}, s32[64,3]{0,1:T(4,128)}, u32[]{:S(2)}) copy-start(s32[64,3]{0,1:T(4,128)} %param.11) | copy-start | bytes 2308
  18.1 448.1 %all-to-all-start = ((bf16[3,4,256,256]{3,2,0,1:T(8,128)(2,1)}), bf16[3,4,256,256]{3,2,0,1:T(8,128)(2,1)S(1)}, u32[]{:S(2)}, u32[]{:S(2)}) async-start(bf16[3,4,256,256]{3,2,0,1:T(8,128)(2,1)} %copy.20), calls=%async_computation | async-start | bytes 3145728 | tf_op jit(solution)/shard_map/all_to_all | solution.py:95
  119.3 2.0 copy-start.2
  436.7 5.6 %copy-start.1 = (f32[1024,1024]{1,0:T(8,128)S(1)}, f32[1024,1024]{1,0:T(8,128)}, u32[]{:S(2)}) copy-start(f32[1024,1024]{1,0:T(8,128)} %fusion.42) | copy-start | bytes 12582916
  485.9 1.1 copy-start.3
  489.4 50.7 %all-to-all-start.1 = ((bf16[3,4,64,1024]{3,1,0,2:T(4,128)(2,1)}), bf16[3,4,64,1024]{3,1,0,2:T(4,128)(2,1)}, u32[]{:S(2)}, u32[]{:S(2)}) async-start(bf16[3,4,64,1024]{3,1,0,2:T(4,128)(2,1)} %copy.24), calls=%async_computation.1 | async-start | bytes 3145728 | tf_op jit(solution)/shard_map/all_to_all | solution.py:120
  500.4 44.4 %all-gather.7.cloned.1.call-start = ((), (), s32[]{:S(2)}) async-start(), calls=%async_computation.3 | async-start | bytes 1310720 | tf_op jit(solution)/shard_map/all_gather | solution.py:39
  544.7 5.9 %copy-start.4 = (f32[128,1,4,1,512]{4,3,2,1,0:T(1,128)S(1)}, f32[128,1,4,1,512]{4,3,2,1,0:T(1,128)}, u32[]{:S(2)}) copy-start(f32[128,1,4,1,512]{4,3,2,1,0:T(1,128)} %param.21) | copy-start | bytes 3145732
Sparse Core Ops, SparseCore 0:
  10.0 51.0 all-gather.4
  63.5 34.2 all-gather.8
  507.3 26.3 all-gather.6
where the time goes:
time: 567 us; the launch traced here: 560 us
  other arithmetic  275 us (49%)
  waiting for transfers between devices  102 us (18%)
  matrix products  95.5 us (17%)
  local copies, waits for them, and re-layouts  50.8 us (9%)
  between operations  20.4 us (4%)
  starting transfers between devices  16.4 us (3%)
    another operation x30, other arithmetic, per_device(): factor = jnp.linalg.cholesky(diag_system)  172 us
    another operation x3, other arithmetic, per_device(): inverse = jax.scipy.linalg.solve_triangular(factor, identity, lower=True)  84.4 us
    all_gather x1, waiting for transfers between devices, per_device(): lax.all_gather(diag_low[None], 'cols', axis=0, tiled=True)  36.7 us
    all_gather x1, waiting for transfers between devices, per_device(): lax.all_gather(diagonal_left_factor[None], 'cols', axis=0, tiled=True)  34 us
    all_to_all x1, waiting for transfers between devices, per_device(): lax.all_to_all(outgoing_rows, 'rows', split_axis=2, concat_axis=2, tiled=...  31.1 us
    another operation x15, matrix products, per_device(): inverse = jax.scipy.linalg.solve_triangular(factor, identity, lower=True)  29.4 us
    another operation x24, local copies, waits for them, and re-layouts  27.4 us
    another operation x14, matrix products, per_device(): factor = jnp.linalg.cholesky(diag_system)  23.3 us
  transfers between devices with their start and end apart: 5, of which 3 were waited for; matrix products, arithmetic and copies ran while one was open for 69% of the time, Pallas kernels for 0%

commit v1 on v0

--- a/solution.py
+++ b/solution.py
@@ -117,7 +117,12 @@
     forward = diag_solution.astype(jnp.bfloat16)
     pick_rows = owner_rows(slot_tile, tile_count, per_peer, row_devices)
     outgoing_rows = panel_factor.reshape(slot_count, per_peer, row_devices, tile_order)
-    incoming = lax.all_to_all(outgoing_rows, "rows", split_axis=2, concat_axis=2, tiled=True)
+    incoming = jnp.concatenate(
+        lax.all_to_all(
+            jnp.stack(jnp.split(outgoing_rows, lax.axis_size("rows"), axis=2)), "rows", 0, 0
+        ),
+        axis=2,
+    )
     owned_rows = jnp.take(incoming.reshape(-1, tile_order), pick_rows, axis=0)
     product = times_block(owned_rows, forward).astype(jnp.bfloat16)
     rhs_out = rhs_rest - product.reshape(rhs_rest.shape).astype(jnp.float32)

time: 567 us -> 608 us (1.072)
  local copies, waits for them, and re-layouts: 50.8 us -> 91.7 us
    unnamed x22 -> x87, local copies, waits for them, and re-layouts: 3.25 us -> 42.1 us
    another operation x24 -> x25, local copies, waits for them, and re-layouts: 27.4 us -> 28 us
  transfers between devices with their start and end apart: 5 -> 5, of which waited for: 3 -> 3; matrix products, arithmetic and copies ran while one was open for 69% -> 64% of each run, Pallas kernels for 0% -> 0%
where the time goes in v1:
time: 608 us; the launch traced here: 601 us
  other arithmetic  275 us (45%)
  waiting for transfers between devices  102 us (17%)
  matrix products  95.8 us (16%)
  local copies, waits for them, and re-layouts  91.7 us (15%)
  between operations  20.6 us (3%)
  starting transfers between devices  15.9 us (3%)
    another operation x30, other arithmetic, per_device(): factor = jnp.linalg.cholesky(diag_system)  172 us
    another operation x3, other arithmetic, per_device(): inverse = jax.scipy.linalg.solve_triangular(factor, identity, lower=True)  84.4 us
    unnamed x87, local copies, waits for them, and re-layouts  42.1 us
    all_gather x1, waiting for transfers between devices, per_device(): lax.all_gather(diag_low[None], 'cols', axis=0, tiled=True)  36.7 us
    all_gather x1, waiting for transfers between devices, per_device(): lax.all_gather(diagonal_left_factor[None], 'cols', axis=0, tiled=True)  34 us
    all_to_all x1, waiting for transfers between devices, per_device(): lax.all_to_all(jnp.stack(jnp.split(outgoing_rows, lax.axis_size('rows'),...  31.4 us
    another operation x15, matrix products, per_device(): inverse = jax.scipy.linalg.solve_triangular(factor, identity, lower=True)  29.4 us
    another operation x24, local copies, waits for them, and re-layouts  27.4 us
  transfers between devices with their start and end apart: 5, of which 3 were waited for; matrix products, arithmetic and copies ran while one was open for 64% of the time, Pallas kernels for 0%

profile of v1, /device:TPU:1, one launch (start us, length us, event | category | flops | bytes accessed | tf_op | source)
XLA Modules:
  0.0 600.7 jit_solution(14431370827330873191)
XLA Ops:
  27.1 34.0 %all-gather.5.cloned.1.call-done = bf16[4,1024,256]{2,1,0:T(8,128)(2,1)} async-done(((bf16[1,1024,256]{2,1,0:T(8,128)(2,1)}), bf16[4,1024,256]{2,1,0:T(8,128)(2,1)}) %all-gather.5.cloned.1.call-update) | async-done | bytes 2097168 | tf_op jit(solution)/shard_map/all_gather | solution.py:90
  61.1 36.7 %all-gather.9.cloned.1.call-done = bf16[4096,256]{1,0:T(8,128)(2,1)} async-done(((bf16[1024,256]{1,0:T(8,128)(2,1)}), bf16[4096,256]{1,0:T(8,128)(2,1)}) %all-gather.9.cloned.1.call-update) | async-done | bytes 2097168 | tf_op jit(solution)/shard_map/all_gather | solution.py:89
  97.8 6.6 %convolution_bitcast_fusion = f32[1024,1024]{1,0:T(8,128)} fusion(bf16[4,1024,256]{2,1,0:T(8,128)(2,1)} %bitcast.435, bf16[4,1024,256]{2,1,0:T(8,128)(2,1)} %all-gather.5.cloned.1.call-done), kind=kOutput, calls=%fused_computation.28 | convolution fusion | flops 2147483648 | bytes 8388608 | tf_op jit(solution)/shard_map/jbr,jcr->bc/dot_general | solution.py:101
  109.7 9.6 %fusion.3 = f32[1024,1024]{1,0:T(8,128)S(1)} fusion(f32[1024,1024]{0,1:T(8,128)} %copy.151, f32[1024,1024]{1,0:T(8,128)} %convolution_bitcast_fusion, f32[1024]{0:T(1024)S(1)} %bitcast.430, f32[1024]{0:T(1024)S(1)} %bitcast.428), kind=kLoop, calls=%fused_computation.9 | loop fusion | flops 33554432 | bytes 12591104 | tf_op jit(solution)/shard_map/jit(cholesky)/div | solution.py:106
  121.3 11.7 %cholesky.224 = f32[128,128]{1,0:T(8,128)S(1)} custom-call(f32[128,128]{1,0:T(8,128)S(1)} %cholesky.583), custom_call_target="Cholesky" | custom-call | tf_op jit(solution)/shard_map/jit(cholesky)/cholesky | solution.py:106
  133.0 9.8 %custom-call.63 = f32[1,128,128]{1,2,0:T(8,128)S(1)} custom-call(f32[1,128,128]{2,1,0:T(8,128)S(1)} %get-tuple-element.131), custom_call_target="InvertDiagBlocksLowerTriangular" | custom-call | tf_op jit(solution)/shard_map/jit(cholesky)/cholesky | solution.py:106
  149.3 11.7 %cholesky.245 = f32[128,128]{1,0:T(8,128)S(1)} custom-call(f32[128,128]{1,0:T(8,128)S(1)} %cholesky.587), custom_call_target="Cholesky" | custom-call | tf_op jit(solution)/shard_map/jit(cholesky)/cholesky | solution.py:106
  161.6 10.2 %custom-call.64 = f32[1,128,128]{1,2,0:T(8,128)S(1)} custom-call(f32[1,128,128]{2,1,0:T(8,128)S(1)} %get-tuple-element.128), custom_call_target="InvertDiagBlocksLowerTriangular" | custom-call | tf_op jit(solution)/shard_map/jit(cholesky)/cholesky | solution.py:106
  175.2 11.7 %cholesky.470 = f32[128,128]{1,0:T(8,128)S(1)} custom-call(f32[128,128]{1,0:T(8,128)S(1)} %cholesky.592), custom_call_target="Cholesky" | custom-call | tf_op jit(solution)/shard_map/jit(cholesky)/cholesky | solution.py:106
  188.3 9.8 %custom-call.65 = f32[1,128,128]{1,2,0:T(8,128)S(1)} custom-call(f32[1,128,128]{2,1,0:T(8,128)S(1)} %get-tuple-element.125), custom_call_target="InvertDiagBlocksLowerTriangular" | custom-call | tf_op jit(solution)/shard_map/jit(cholesky)/cholesky | solution.py:106
  201.6 11.9 %cholesky.489 = f32[128,128]{1,0:T(8,128)S(1)} custom-call(f32[128,128]{1,0:T(8,128)S(1)} %cholesky.597), custom_call_target="Cholesky" | custom-call | tf_op jit(solution)/shard_map/jit(cholesky)/cholesky | solution.py:106
  214.8 9.8 %custom-call.66 = f32[1,128,128]{1,2,0:T(8,128)S(1)} custom-call(f32[1,128,128]{2,1,0:T(8,128)S(1)} %get-tuple-element.122), custom_call_target="InvertDiagBlocksLowerTriangular" | custom-call | tf_op jit(solution)/shard_map/jit(cholesky)/cholesky | solution.py:106
  228.1 11.7 %cholesky.508 = f32[128,128]{1,0:T(8,128)S(1)} custom-call(f32[128,128]{1,0:T(8,128)S(1)} %cholesky.602), custom_call_target="Cholesky" | custom-call | tf_op jit(solution)/shard_map/jit(cholesky)/cholesky | solution.py:106
  241.1 9.8 %custom-call.67 = f32[1,128,128]{1,2,0:T(8,128)S(1)} custom-call(f32[1,128,128]{2,1,0:T(8,128)S(1)} %get-tuple-element.119), custom_call_target="InvertDiagBlocksLowerTriangular" | custom-call | tf_op jit(solution)/shard_map/jit(cholesky)/cholesky | solution.py:106
  254.4 11.7 %cholesky.528 = f32[128,128]{1,0:T(8,128)S(1)} custom-call(f32[128,128]{1,0:T(8,128)S(1)} %cholesky.607), custom_call_target="Cholesky" | custom-call | tf_op jit(solution)/shard_map/jit(cholesky)/cholesky | solution.py:106
  267.5 9.8 %custom-call.68 = f32[1,128,128]{1,2,0:T(8,128)S(1)} custom-call(f32[1,128,128]{2,1,0:T(8,128)S(1)} %get-tuple-element.116), custom_call_target="InvertDiagBlocksLowerTriangular" | custom-call | tf_op jit(solution)/shard_map/jit(cholesky)/cholesky | solution.py:106
  280.3 11.7 %cholesky.548 = f32[128,128]{1,0:T(8,128)S(1)} custom-call(f32[128,128]{1,0:T(8,128)S(1)} %cholesky.612), custom_call_target="Cholesky" | custom-call | tf_op jit(solution)/shard_map/jit(cholesky)/cholesky | solution.py:106
  293.3 10.2 %custom-call.69 = f32[1,128,128]{1,2,0:T(8,128)S(1)} custom-call(f32[1,128,128]{2,1,0:T(8,128)S(1)} %get-tuple-element.113), custom_call_target="InvertDiagBlocksLowerTriangular" | custom-call | tf_op jit(solution)/shard_map/jit(cholesky)/cholesky | solution.py:106
  306.2 11.7 %cholesky.566 = f32[128,128]{1,0:T(8,128)S(1)} custom-call(f32[128,128]{1,0:T(8,128)S(1)} %convolution_subtract_fusion.11), custom_call_target="Cholesky" | custom-call | tf_op jit(solution)/shard_map/jit(cholesky)/cholesky | solution.py:106
  329.7 27.4 %while.1 = (s32[]{:T(128)}, f32[1024,1024]{1,0:T(8,128)}, s32[8,2]{0,1:T(2,128)S(1)}, f32[8,128,128]{2,1,0:T(8,128)}, s32[]{:T(128)}) while((s32[]{:T(128)}, f32[1024,1024]{1,0:T(8,128)}, s32[8,2]{0,1:T(2,128)S(1)}, f32[8,128,128]{2,1,0:T(8,128)}, s32[]{:T(128)}) %tuple.126), condition=%wide.while_cond, body=%wide.while_body.sunk | while | flops 2 | bytes 132705 | solution.py:107
  357.1 79.6 %custom-call.70 = f32[8,128,128]{1,2,0:T(8,128)S(1)} custom-call(f32[8,128,128]{2,1,0:T(8,128)} %get-tuple-element.10), custom_call_target="InvertDiagBlocksLowerTriangular" | custom-call | tf_op jit(solution)/shard_map/jit(_solve_triangular)/triangular_solve | solution.py:107
  469.6 16.5 %fusion.29 = bf16[3,256,1024]{2,1,0:T(8,128)(2,1)S(1)} fusion(f32[1024,1024]{1,0:T(8,128)} %convolution_dynamic-update-slice_fusion, f32[3,256,1024,1]{2,1,0,3:T(8,128)S(1)} %fusion.27, f32[1024]{0:T(1024)S(1)} %bitcast.431, f32[3,256]{1,0:T(4,128)S(1)} %get-tuple-element.148, f32[1024]{0:T(1024)S(1)} %bitcast.429, f32[3,256]{1,0:T(4,128)S(1)} %get-tuple-element.149, ...), kind=kOutput, calls=%fused_computation.40 | convolution fusion | flops 9674686464 | bytes 8927244 | tf_op jit(solution)/shard_map/snb,cb->snc/dot_general | solution.py:113
  529.1 10.8 %all-to-all-start.1 = ((bf16[64,3,4,1,1024]{4,2,1,3,0:T(4,128)(2,1)}), bf16[64,3,4,1,1024]{4,2,1,3,0:T(4,128)(2,1)S(1)}, u32[]{:S(2)}, u32[]{:S(2)}) async-start(bf16[64,3,4,1,1024]{4,2,1,3,0:T(4,128)(2,1)} %constant_dynamic-update-slice_fusion.25), calls=%async_computation.1 | async-start | bytes 3145728 | tf_op jit(solution)/shard_map/all_to_all | solution.py:121
  548.3 31.4 %all-to-all-done.1 = bf16[64,3,4,1,1024]{4,2,1,3,0:T(4,128)(2,1)S(1)} async-done(((bf16[64,3,4,1,1024]{4,2,1,3,0:T(4,128)(2,1)}), bf16[64,3,4,1,1024]{4,2,1,3,0:T(4,128)(2,1)S(1)}, u32[]{:S(2)}, u32[]{:S(2)}) %all-to-all-start.1) | async-done | bytes 1572896 | tf_op jit(solution)/shard_map/all_to_all | solution.py:121
  (213 shorter events, 191.7 us)
Async XLA Ops:
  7.2 532.8 %copy-start = (f32[1024,128]{1,0:T(8,128)S(1)}, f32[1024,128]{1,0:T(8,128)}, u32[]{:S(2)}) copy-start(f32[1024,128]{1,0:T(8,128)} %param.20) | copy-start | bytes 1572868
  7.2 5.9 copy-start.10
  7.2 5.8 copy-start.9
  7.2 53.9 %all-gather.5.cloned.1.call-start = ((), (), s32[]{:S(2)}) async-start(), calls=%async_computation.2 | async-start | bytes 2621440 | tf_op jit(solution)/shard_map/all_gather | solution.py:90
  9.9 87.9 %all-gather.9.cloned.1.call-start = ((), (), s32[]{:S(2)}) async-start(), calls=%async_computation.4 | async-start | bytes 2621440 | tf_op jit(solution)/shard_map/all_gather | solution.py:89
  16.8 6.3 %copy-start.7 = (s32[2,1024]{1,0:T(2,128)S(1)}, s32[2,1024]{1,0:T(2,128)}, u32[]{:S(2)}) copy-start(s32[2,1024]{1,0:T(2,128)} %param.19) | copy-start | bytes 24580
  16.8 6.3 %copy-start.8 = (s32[3,2,256]{2,1,0:T(2,128)S(1)}, s32[3,2,256]{2,1,0:T(2,128)}, u32[]{:S(2)}) copy-start(s32[3,2,256]{2,1,0:T(2,128)} %param.18) | copy-start | bytes 18436
  16.8 6.3 %copy-start.6 = (s32[64,3]{0,1:T(4,128)S(1)}, s32[64,3]{0,1:T(4,128)}, u32[]{:S(2)}) copy-start(s32[64,3]{0,1:T(4,128)} %param.11) | copy-start | bytes 2308
  18.1 448.0 %all-to-all-start = ((bf16[3,4,256,256]{3,2,0,1:T(8,128)(2,1)}), bf16[3,4,256,256]{3,2,0,1:T(8,128)(2,1)S(1)}, u32[]{:S(2)}, u32[]{:S(2)}) async-start(bf16[3,4,256,256]{3,2,0,1:T(8,128)(2,1)} %copy.149), calls=%async_computation | async-start | bytes 3145728 | tf_op jit(solution)/shard_map/all_to_all | solution.py:95
  119.3 2.0 copy-start.2
  438.9 3.4 copy-start.1
  486.1 3.5 copy-start.3
  529.1 50.6 %all-to-all-start.1 = ((bf16[64,3,4,1,1024]{4,2,1,3,0:T(4,128)(2,1)}), bf16[64,3,4,1,1024]{4,2,1,3,0:T(4,128)(2,1)S(1)}, u32[]{:S(2)}, u32[]{:S(2)}) async-start(bf16[64,3,4,1,1024]{4,2,1,3,0:T(4,128)(2,1)} %constant_dynamic-update-slice_fusion.25), calls=%async_computation.1 | async-start | bytes 3145728 | tf_op jit(solution)/shard_map/all_to_all | solution.py:121
  539.9 45.9 %all-gather.7.cloned.1.call-start = ((), (), s32[]{:S(2)}) async-start(), calls=%async_computation.3 | async-start | bytes 1310720 | tf_op jit(solution)/shard_map/all_gather | solution.py:39
  579.7 1.2 copy-start.4
  585.8 5.9 copy-start.5
Sparse Core Ops, SparseCore 0:
  10.0 51.0 all-gather.4
  63.5 34.2 all-gather.8
  546.6 26.3 all-gather.6
